TPU v7x, 32 devices: a whole 2x2x4 slice. The times are simulated.
32 devices in a mesh: cfg: 2 (over core), seq: 8 (over z, y), mlp: 2 (over x).
Axes of the slice: x: 2, y: 2, z: 4, core: 2. Of those that a mesh axis runs over, the one named last changes fastest.
Arguments:
- image_hidden: bfloat16 [2, 256, 8, 1536], P('cfg', ('seq', 'mlp')), may hold values from -6 to 6
- text_hidden: bfloat16 [2, 1232, 1536], P('cfg', 'seq'), may hold values from -6 to 6
- modulation: float32 [2, 8, 10, 1536], P('cfg'), may hold values from -3 to 3
- text_lengths: int32 [2, 8], P('cfg'), may hold values from 1 to 154, as said below
- timestep: int32 [1], replicated, may hold values from 0 to 27
- latent: float32 [256, 8, 64], P(('seq', 'mlp'), 'cfg'), may hold values from -6 to 6
- w_qkv: bfloat16 [3, 1536, 1536], P(None, None, 'mlp'), may hold values from -0.15625 to 0.15625
- w_out: bfloat16 [1536, 1536], P('mlp'), may hold values from -0.15625 to 0.15625
- w_text_kv: bfloat16 [2, 1536, 1536], P(None, None, 'mlp'), may hold values from -0.15625 to 0.15625
- norm_gain: float32 [3, 64], replicated, may hold values from 1 to 2
- w_up: bfloat16 [1536, 6144], P(None, 'mlp'), may hold values from -0.15625 to 0.15625
- w_down: bfloat16 [6144, 1536], P('mlp'), may hold values from -0.078125 to 0.078125
- w_head: bfloat16 [1536, 64], replicated, may hold values from -0.078125 to 0.078125
Outputs:
- velocity: float32 [256, 8, 64], P(('seq', 'mlp'), 'cfg')
- next_latent: float32 [256, 8, 64], P(('seq', 'mlp'), 'cfg')
- denoised: float32 [256, 8, 64], P(('seq', 'mlp'), 'cfg')
Inputs may be any that keep to these rules, and one draw needn't show every extreme that they name: Text position j of prompt b in half c is a real token only if j < text_lengths[c, b]; in every draw some length equals 154 and some equals 1.
All inputs are finite; a program needn't handle non-finite values.
Results may differ from a plain program's by a relative error of at most 0.0085.
Values may be sent and summed in bfloat16 or wider, within the bound.
A program may use at most 128 MiB of HBM per device.

v0:
```python
import math

import jax
import jax.numpy as jnp
from jax import lax
from jax.sharding import PartitionSpec as P

HEAD_DIM = 64
TXT = 154
STEPS = 28


EPS = 1e-06
GUIDE = 4.5
SHIFT = 3.0


def partner_2(block, axis, stride):
    count = lax.axis_size(axis)
    route = []
    for low in range(count):
        high = low | 1 << stride
        if high != low and high < count:
            route += [(low, high), (high, low)]
    return lax.ppermute(block, axis, route)


def layer_norm(values):
    mean = jnp.mean(values, axis=-1, keepdims=True)
    centred = values - mean
    spread = jnp.mean(centred * centred, axis=-1, keepdims=True)
    return centred * lax.rsqrt(spread + EPS)


def modulate(values, shift, scale):
    return layer_norm(values) * (1.0 + scale) + shift


def head_norm(values, gain):
    shaped = values.reshape(values.shape[:-1] + (values.shape[-1] // HEAD_DIM, HEAD_DIM))
    square = jnp.mean(shaped * shaped, axis=-1, keepdims=True)
    return (shaped * lax.rsqrt(square + EPS) * gain).astype(jnp.bfloat16)


def sigma_of(index):
    level = 1.0 - index.astype(jnp.float32) / STEPS
    return SHIFT * level / (1.0 + (SHIFT - 1.0) * level)


def project_image(normed_rows, w_qkv, norm_gain):
    query = head_norm(
        jnp.einsum("tbd,de->tbe", normed_rows, w_qkv[0], preferred_element_type=jnp.float32),
        norm_gain[0],
    )
    keys = head_norm(
        jnp.einsum("tbd,de->tbe", normed_rows, w_qkv[1], preferred_element_type=jnp.float32),
        norm_gain[1],
    )
    values = jnp.einsum(
        "tbd,de->tbe", normed_rows, w_qkv[2], preferred_element_type=jnp.float32
    ).astype(jnp.bfloat16)
    flat_query = query.reshape(query.shape[:-2] + (-1,))
    flat_keys = keys.reshape(keys.shape[:-2] + (-1,))
    return jnp.concatenate([flat_query, flat_keys, values], axis=-1)


def key_terms(query, key_rows, value_rows, keep):
    factor = 1.0 / math.sqrt(HEAD_DIM)
    prompts = query.shape[1]
    if keep is None:
        keep = jnp.ones((prompts, key_rows.shape[0]), jnp.float32)

    def one_prompt(items):
        query_rows, keys_one, values_one, keep_one = items
        scores = (
            jnp.einsum("qhd,khd->hqk", query_rows, keys_one, preferred_element_type=jnp.float32)
            * factor
        )
        weights = jnp.exp(scores) * keep_one[None, None, :]
        numer = jnp.einsum(
            "hqk,khd->hqd",
            weights.astype(jnp.bfloat16),
            values_one,
            preferred_element_type=jnp.float32,
        )
        return (numer, jnp.sum(weights, axis=-1))

    return lax.map(
        one_prompt,
        (
            jnp.moveaxis(query, 1, 0),
            jnp.moveaxis(key_rows, 1, 0),
            jnp.moveaxis(value_rows, 1, 0),
            keep,
        ),
    )


def shards(
    image_hidden,
    text_hidden,
    modulation,
    text_lengths,
    timestep,
    latent,
    w_qkv,
    w_out,
    w_text_kv,
    norm_gain,
    w_up,
    w_down,
    w_head,
):
    mods = modulation[0]
    own_hidden = image_hidden[0]
    rows = own_hidden.shape[0]
    width = w_out.shape[0]
    heads = width // HEAD_DIM
    prompts = mods.shape[0]
    offset = lax.axis_index("mlp") * rows
    block_hidden = lax.all_gather(own_hidden, "mlp", axis=0, tiled=True).astype(jnp.float32)
    normed = modulate(block_hidden, mods[:, 0], mods[:, 1]).astype(jnp.bfloat16)
    projected = project_image(normed, w_qkv, norm_gain)
    block_rows = projected.shape[0]
    query = projected[..., :width].reshape(block_rows, prompts, heads, HEAD_DIM)
    own_pairs = projected[..., width:]
    text_rows = text_hidden.shape[1]
    position = lax.axis_index("seq") * text_rows + lax.iota(jnp.int32, text_rows)
    owner = position // TXT
    pick = (owner[:, None] == lax.iota(jnp.int32, prompts)[None, :]).astype(jnp.float32)
    text_shift = jnp.dot(pick, mods[:, 6], precision=lax.Precision.HIGHEST)
    text_scale = jnp.dot(pick, mods[:, 7], precision=lax.Precision.HIGHEST)
    text_normed = modulate(text_hidden[0].astype(jnp.float32), text_shift, text_scale).astype(
        jnp.bfloat16
    )
    text_keys = head_norm(
        jnp.dot(text_normed, w_text_kv[0], preferred_element_type=jnp.float32), norm_gain[2]
    )
    text_keys = text_keys.reshape(text_rows, width)
    text_values = jnp.dot(text_normed, w_text_kv[1], preferred_element_type=jnp.float32).astype(
        jnp.bfloat16
    )
    text_pairs = jnp.concatenate([text_keys, text_values], axis=-1)
    keep = (lax.iota(jnp.int32, TXT)[None, :] < text_lengths[0][:, None]).astype(jnp.float32)

    def split_pairs(pairs):
        shape = pairs.shape[:2] + (heads, HEAD_DIM)
        return (pairs[..., :width].reshape(shape), pairs[..., width:].reshape(shape))

    all_image, all_text = (
        lax.all_gather(own_pairs, "seq", axis=0, tiled=True),
        lax.all_gather(text_pairs, "seq", axis=0, tiled=True),
    )
    shaped = jnp.transpose(all_text.reshape(prompts, TXT, 2 * width), (1, 0, 2))
    key_rows, value_rows = split_pairs(shaped)
    text_numer, text_denom = key_terms(query, key_rows, value_rows, keep)
    key_rows, value_rows = split_pairs(all_image)
    image_numer, image_denom = key_terms(query, key_rows, value_rows, None)
    numer = text_numer + image_numer
    denom = text_denom + image_denom
    attended = (numer / denom[..., None]).astype(jnp.bfloat16)
    attended = jnp.transpose(attended, (2, 0, 1, 3)).reshape(block_rows, prompts, width)
    part = attended
    attention_out = lax.psum(
        jnp.einsum("tbe,ed->tbd", part, w_out, preferred_element_type=jnp.float32).astype(
            jnp.bfloat16
        ),
        "mlp",
    ).astype(jnp.float32)
    first = block_hidden + mods[:, 2] * attention_out
    mlp_in = modulate(first, mods[:, 3], mods[:, 4]).astype(jnp.bfloat16)
    raised = jnp.einsum("tbd,du->tbu", mlp_in, w_up, preferred_element_type=jnp.float32)
    activated = jax.nn.gelu(raised, approximate=True).astype(jnp.bfloat16)
    own_first = lax.dynamic_slice_in_dim(first, offset, rows, 0)
    part = activated
    mlp_out = lax.psum_scatter(
        jnp.einsum("tbu,ud->tbd", part, w_down, preferred_element_type=jnp.float32).astype(
            jnp.bfloat16
        ),
        "mlp",
        scatter_dimension=0,
        tiled=True,
    ).astype(jnp.float32)
    second = own_first + mods[:, 5] * mlp_out
    final = modulate(second, mods[:, 8], mods[:, 9]).astype(jnp.bfloat16)
    own_velocity = jnp.einsum("tbd,dp->tbp", final, w_head, preferred_element_type=jnp.float32)
    half_count = prompts // 2
    branch = lax.axis_index("cfg")
    outgoing = lax.dynamic_slice_in_dim(own_velocity, (1 - branch) * half_count, half_count, 1)
    kept = lax.dynamic_slice_in_dim(own_velocity, branch * half_count, half_count, 1)
    partner = partner_2(outgoing, "cfg", 0)
    is_conditional = branch == 0
    conditional = jnp.where(is_conditional, kept, partner)
    unconditional = jnp.where(is_conditional, partner, kept)
    velocity = unconditional + GUIDE * (conditional - unconditional)
    sigma_now = sigma_of(timestep[0])
    sigma_after = sigma_of(timestep[0] + 1)
    next_latent = latent + (sigma_after - sigma_now) * velocity
    denoised = latent - sigma_now * velocity
    return (velocity, next_latent, denoised)


def solution(mesh):
    placed = (
        P("cfg", ("seq", "mlp"), None, None),
        P("cfg", "seq", None),
        P("cfg", None, None, None),
        P("cfg", None),
        P(),
        P(("seq", "mlp"), "cfg", None),
        P(None, None, "mlp"),
        P("mlp", None),
        P(None, None, "mlp"),
        P(),
        P(None, "mlp"),
        P("mlp", None),
        P(),
    )
    return jax.shard_map(
        shards,
        mesh=mesh,
        in_specs=placed,
        out_specs=(
            P(("seq", "mlp"), "cfg", None),
            P(("seq", "mlp"), "cfg", None),
            P(("seq", "mlp"), "cfg", None),
        ),
        check_vma=False,
    )
```

profile of v0, /device:TPU:1, one launch (start us, length us, event | category | flops | bytes accessed | tf_op | source)
XLA Modules:
  0.0 328.5 jit_solution(14662058543458932708)
XLA Ops:
  14.3 3.2 slice_bitcast_fusion.1
  17.5 4.3 %copy.71 = bf16[768,1536]{1,0:T(8,128)(2,1)} copy(bf16[768,1536]{0,1:T(8,128)(2,1)} %slice_bitcast_fusion.1) | data formatting | bytes 4718592 | tf_op jit(solution)/shard_map/dot_general | solution.py:137
  21.8 2.4 fusion.64
  26.2 4.8 %slice_bitcast_fusion = (bf16[768,1536]{0,1:T(8,128)(2,1)}, bf16[768,1536]{0,1:T(8,128)(2,1)}) fusion(bf16[3,1536,768]{2,1,0:T(8,128)(2,1)} %param.23), kind=kLoop, calls=%fused_computation.55 | loop fusion | bytes 9437184 | tf_op jit(solution)/shard_map/tbd,de->tbe/dot_general | solution.py:56
  31.1 4.4 %copy.75 = bf16[768,1536]{1,0:T(8,128)(2,1)} copy(bf16[768,1536]{0,1:T(8,128)(2,1)} %get-tuple-element.177) | data formatting | bytes 4718592 | tf_op jit(solution)/shard_map/tbd,de->tbe/dot_general | solution.py:56
  35.4 11.8 %all-gather = bf16[1,32,8,1536]{3,2,0,1:T(8,128)(2,1)S(1)} all-gather(bf16[1,16,8,1536]{3,2,0,1:T(8,128)(2,1)S(1)} %bitcast.270), channel_id=2, replica_groups=mesh['cfg'=2,'seq'=8,'mlp'=2] {'mlp'}, dimensions={1}, use_global_device_ids=true | all-gather | bytes 1179648 | tf_op jit(solution)/shard_map/all_gather | solution.py:121
  48.5 2.7 multiply_reduce_fusion.1
  56.7 2.6 fusion.61
  60.5 4.3 %copy.68 = bf16[768,1536]{1,0:T(8,128)(2,1)} copy(bf16[768,1536]{0,1:T(8,128)(2,1)} %get-tuple-element.178) | data formatting | bytes 4718592 | tf_op jit(solution)/shard_map/tbd,de->tbe/dot_general | solution.py:52
  64.8 4.3 %multiply_reduce_fusion.2 = (f32[32,8,12]{1,2,0:T(8,128)S(1)}, f32[32,8,12,64]{3,1,2,0:T(8,128)}) fusion(bf16[12,64,1536,1]{2,1,0,3:T(8,128)(2,1)} %bitcast.264, f32[8,1536]{1,0:T(8,128)S(1)} %copy-done.16, f32[8,1536]{1,0:T(8,128)S(1)} %copy-done.18, f32[32,8]{1,0:T(8,128)S(1)} %copy-done.20, f32[32,8]{1,0:T(8,128)S(1)} %broadcast_multiply_fusion.1, ...), kind=kOutput, calls=%fused_computation.77 | convolution fusion | flops 606729216 | bytes 4044800 | tf_op jit(solution)/shard_map/tbd,de->tbe/dot_general | solution.py:52
  72.6 24.8 %all-gather.7.cloned.1.call-done = bf16[8,154,1536]{2,1,0:T(8,128)(2,1)} async-done(((bf16[1,154,1536]{2,1,0:T(8,128)(2,1)}), bf16[8,154,1536]{2,1,0:T(8,128)(2,1)}) %all-gather.7.cloned.1.call-update) | async-done | bytes 3784720 | tf_op jit(solution)/shard_map/all_gather | solution.py:152
  97.4 7.8 %copy.73 = bf16[8,154,1536]{1,2,0:T(8,128)(2,1)} copy(bf16[8,154,1536]{2,1,0:T(8,128)(2,1)} %all-gather.7.cloned.1.call-done) | data formatting | bytes 7569408 | tf_op jit(solution)/shard_map/all_gather | solution.py:152
  105.2 6.5 %fusion.100 = (bf16[154,8,768]{0,2,1:T(8,128)(2,1)}, bf16[154,8,768]{0,2,1:T(8,128)(2,1)}) fusion(bf16[154,8,1536]{0,2,1:T(8,128)(2,1)} %bitcast.258), kind=kLoop, calls=%fused_computation.149 | loop fusion | bytes 7569408 | tf_op jit(solution)/shard_map/slice | solution.py:148
  113.0 26.2 %while.24 = (s32[]{:T(128)}, f32[8,12,32,64]{3,2,1,0:T(8,128)}, f32[8,12,32]{2,1,0:T(8,128)S(1)}, bf16[8,32,12,64]{3,1,2,0:T(8,128)(2,1)}, bf16[8,154,12,64]{1,3...) while((s32[]{:T(128)}, f32[8,12,32,64]{3,2,1,0:T(8,128)}, ...), condition=%wide.region_8.9_spmd, body=%wide.region_6.8_spmd.sunk | while | flops 15374978 | bytes 1339797 | solution.py:88
  114.4 1.9 fusion.120
  117.7 1.9 fusion.120
  127.5 1.9 fusion.120
  130.8 1.9 fusion.120
  134.1 1.9 fusion.120
  139.2 58.3 %all-gather.5.cloned.1.call-done = bf16[256,8,1536]{2,1,0:T(8,128)(2,1)} async-done(((bf16[32,8,1536]{2,1,0:T(8,128)(2,1)}), bf16[256,8,1536]{2,1,0:T(8,128)(2,1)}) %all-gather.5.cloned.1.call-update) | async-done | bytes 6291472 | tf_op jit(solution)/shard_map/all_gather | solution.py:151
  197.6 5.9 %fusion.99 = (bf16[256,8,768]{2,1,0:T(8,128)(2,1)}, bf16[256,8,768]{2,1,0:T(8,128)(2,1)}) fusion(bf16[256,8,1536]{2,1,0:T(8,128)(2,1)} %all-gather.5.cloned.1.call-done), kind=kLoop, calls=%fused_computation.148 | loop fusion | bytes 12582912 | tf_op jit(solution)/shard_map/slice | solution.py:148
  203.5 5.0 %copy.84 = bf16[256,8,768]{0,2,1:T(8,128)(2,1)} copy(bf16[256,8,768]{2,1,0:T(8,128)(2,1)} %get-tuple-element.180) | data formatting | bytes 6291456
  208.4 5.0 %copy.85 = bf16[256,8,768]{0,2,1:T(8,128)(2,1)} copy(bf16[256,8,768]{2,1,0:T(8,128)(2,1)} %get-tuple-element.179) | data formatting | bytes 6291456
  214.8 26.0 %while.25 = (s32[]{:T(128)}, f32[8,12,32,64]{3,2,1,0:T(8,128)}, f32[8,12,32]{2,1,0:T(8,128)S(1)}, bf16[8,32,12,64]{3,1,2,0:T(8,128)(2,1)}, bf16[8,256,12,64]{1,3...) while((s32[]{:T(128)}, f32[8,12,32,64]{3,2,1,0:T(8,128)}, f32[8,12,32]{2,1,0:T(8,128)S(1)}, ...), condition=%wide.region_12.13_spmd, body=%wide.region_10.12_spmd.sunk | while | flops 25460352 | bytes 1494609 | solution.py:88
  219.4 1.9 fusion.124
  222.6 1.9 fusion.124
  229.1 1.9 fusion.124
  240.8 2.4 fusion.79
  248.4 32.9 %all-reduce.2.cloned.1.call-done = bf16[32,8,1536]{2,1,0:T(8,128)(2,1)} async-done(((bf16[32,8,1536]{2,1,0:T(8,128)(2,1)}), bf16[32,8,1536]{2,1,0:T(8,128)(2,1)}) %all-reduce.2.cloned.1.call-update) | async-done | bytes 786448 | tf_op jit(solution)/shard_map/psum | solution.py:164
  283.7 7.0 %fusion.36 = bf16[32,8,3072]{2,1,0:T(8,128)(2,1)S(1)} fusion(bf16[1536,3072]{1,0:T(8,128)(2,1)} %param.27, f32[32,8,1536]{2,1,0:T(8,128)S(1)} %get-tuple-element.172, f32[8,1536]{1,0:T(8,128)S(1)} %copy-done.13, f32[8,1536]{1,0:T(8,128)S(1)} %copy-done.14, f32[32,8]{1,0:T(8,128)S(1)} %add_rsqrt_fusion.1, f32[32,8]{1,0:T(8,128)S(1)} %broadcast_multiply_fusion), kind=kOutput, calls=%fused_computation.42 | convolution fusion | flops 2424963072 | bytes 12683264 | tf_op jit(solution)/shard_map/tbd,du->tbu/dot_general | solution.py:172
  290.7 7.2 %fusion.39 = bf16[32,8,1536]{2,1,0:T(8,128)(2,1)} fusion(bf16[32,8,3072]{2,1,0:T(8,128)(2,1)S(1)} %fusion.36, bf16[3072,1536]{1,0:T(8,128)(2,1)} %param.28), kind=kOutput, calls=%fused_computation.43 | convolution fusion | flops 2416312320 | bytes 11796480 | tf_op jit(solution)/shard_map/tbu,ud->tbd/dot_general | solution.py:177
  298.0 17.6 %reduce-scatter.2.cloned.1.call-done = bf16[16,8,1536]{2,1,0:T(8,128)(2,1)} async-done(((bf16[32,8,1536]{2,1,0:T(8,128)(2,1)}), bf16[16,8,1536]{2,1,0:T(8,128)(2,1)}) %reduce-scatter.2.cloned.1.call-update) | async-done | bytes 393232 | tf_op jit(solution)/shard_map/reduce_scatter | solution.py:176
  (159 shorter events, 73.0 us)
Async XLA Ops:
  7.2 239.2 %copy-start = (bf16[768,1536]{1,0:T(8,128)(2,1)S(1)}, bf16[768,1536]{1,0:T(8,128)(2,1)}, u32[]{:S(2)}) copy-start(bf16[768,1536]{1,0:T(8,128)(2,1)} %param.24) | copy-start | bytes 7077892
  7.2 90.2 %all-gather.7.cloned.1.call-start = ((), (), s32[]{:S(2)}) async-start(), calls=%async_computation.4 | async-start | bytes 4423680 | tf_op jit(solution)/shard_map/all_gather | solution.py:152
  21.8 2.4 copy-start.4
  26.2 171.4 %all-gather.5.cloned.1.call-start = ((), (), s32[]{:S(2)}) async-start(), calls=%async_computation.1 | async-start | bytes 7077888 | tf_op jit(solution)/shard_map/all_gather | solution.py:151
  31.1 4.4 %copy-start.8 = (bf16[1,16,8,1536]{3,2,1,0:T(8,128)(2,1)S(1)}, bf16[1,16,8,1536]{3,2,1,0:T(8,128)(2,1)}, u32[]{:S(2)}) copy-start(bf16[1,16,8,1536]{3,2,1,0:T(8,128)(2,1)} %param.17) | copy-start | bytes 1179652
  35.4 12.4 %copy-start.6 = (f32[1,8,10,1536]{3,1,2,0:T(8,128)S(1)}, f32[1,8,10,1536]{3,1,2,0:T(8,128)}, u32[]{:S(2)}) copy-start(f32[1,8,10,1536]{3,1,2,0:T(8,128)} %param.19) | copy-start | bytes 1474564
  35.4 13.1 %copy-start.3 = (bf16[768,1536]{1,0:T(8,128)(2,1)S(1)}, bf16[768,1536]{1,0:T(8,128)(2,1)}, u32[]{:S(2)}) copy-start(bf16[768,1536]{1,0:T(8,128)(2,1)} %copy.75) | copy-start | bytes 7077892
  47.8 3.5 %copy-start.19 = (f32[32,8]{1,0:T(8,128)}, f32[32,8]{1,0:T(8,128)S(1)}, u32[]{:S(2)}) copy-start(f32[32,8]{1,0:T(8,128)S(1)} %add_rsqrt_fusion.3) | copy-start | bytes 3076
  48.5 2.7 copy-start.15
  48.5 2.7 copy-start.17
  48.5 3.1 copy-start.22
  60.2 221.0 %all-reduce.2.cloned.1.call-start = ((), (), s32[]{:S(2)}) async-start(), calls=%async_computation.2 | async-start | bytes 1572864 | tf_op jit(solution)/shard_map/psum | solution.py:164
  60.5 4.3 %copy-start.16 = (f32[8,1536]{1,0:T(8,128)S(1)}, f32[8,1536]{1,0:T(8,128)}, u32[]{:S(2)}) copy-start(f32[8,1536]{1,0:T(8,128)} %copy-done.15) | copy-start | bytes 147460
  60.5 4.3 %copy-start.18 = (f32[8,1536]{1,0:T(8,128)S(1)}, f32[8,1536]{1,0:T(8,128)}, u32[]{:S(2)}) copy-start(f32[8,1536]{1,0:T(8,128)} %copy-done.17) | copy-start | bytes 147460
  60.5 4.3 %copy-start.20 = (f32[32,8]{1,0:T(8,128)S(1)}, f32[32,8]{1,0:T(8,128)}, u32[]{:S(2)}) copy-start(f32[32,8]{1,0:T(8,128)} %copy-done.19) | copy-start | bytes 3076
  64.8 4.6 %copy-start.21 = (f32[64]{0:T(128)S(1)}, f32[64]{0:T(128)}, u32[]{:S(2)}) copy-start(f32[64]{0:T(128)} %get-tuple-element.192) | copy-start | bytes 772
  69.4 3.1 copy-start.23
  248.1 67.4 %reduce-scatter.2.cloned.1.call-start = ((), (), s32[]{:S(2)}) async-start(), calls=%async_computation.3 | async-start | bytes 1179648 | tf_op jit(solution)/shard_map/reduce_scatter | solution.py:176
  282.8 7.9 %copy-start.1 = (f32[32,8,1536]{2,1,0:T(8,128)}, f32[32,8,1536]{2,1,0:T(8,128)S(1)}, u32[]{:S(2)}) copy-start(f32[32,8,1536]{2,1,0:T(8,128)S(1)} %get-tuple-element.172) | copy-start | bytes 4718596
  282.8 0.8 copy-start.13
  282.8 0.9 copy-start.14
  290.7 24.9 %copy-start.7 = (f32[8,1536]{1,0:T(8,128)S(1)}, f32[8,1536]{1,0:T(8,128)}, u32[]{:S(2)}) copy-start(f32[8,1536]{1,0:T(8,128)} %get-tuple-element.183) | copy-start | bytes 147460
  297.9 20.7 %copy-start.11 = (f32[8,1536]{1,0:T(8,128)S(1)}, f32[8,1536]{1,0:T(8,128)}, u32[]{:S(2)}) copy-start(f32[8,1536]{1,0:T(8,128)} %get-tuple-element.184) | copy-start | bytes 147460
  297.9 20.7 %copy-start.12 = (f32[8,1536]{1,0:T(8,128)S(1)}, f32[8,1536]{1,0:T(8,128)}, u32[]{:S(2)}) copy-start(f32[8,1536]{1,0:T(8,128)} %get-tuple-element.185) | copy-start | bytes 147460
  297.9 20.7 %copy-start.24 = (bf16[1536,64]{0,1:T(8,128)(2,1)S(1)}, bf16[1536,64]{0,1:T(8,128)(2,1)}, u32[]{:S(2)}) copy-start(bf16[1536,64]{0,1:T(8,128)(2,1)} %param.29) | copy-start | bytes 589828
  315.6 3.1 copy-start.2
  315.6 3.1 copy-start.5
  317.1 3.5 %copy-start.9 = (f32[16,4,64]{2,1,0:T(4,128)S(1)}, f32[16,4,64]{2,1,0:T(4,128)}, u32[]{:S(2)}) copy-start(f32[16,4,64]{2,1,0:T(4,128)} %param.22) | copy-start | bytes 49156
  319.1 1.6 collective-permute-start
  321.3 0.6 copy-start.10
Sparse Core Ops, SparseCore 0:
  26.3 71.0 all-gather.6
  99.6 97.9 all-gather.4
  248.2 32.9 all-reduce.1
  298.1 17.4 reduce-scatter.1
where the time goes:
time: 331 us; the launch traced here: 328 us
  waiting for transfers between devices  134 us (40%)
  matrix products  84.1 us (25%)
  local copies, waits for them, and re-layouts  64.2 us (19%)
  other arithmetic  18.2 us (5%)
  between operations  14.9 us (5%)
  blocking collectives  11.8 us (4%)
    all_gather x1, waiting for transfers between devices, shards(): lax.all_gather(own_pairs, 'seq', axis=0, tiled=True)  58.3 us
    psum x1, waiting for transfers between devices, shards(): lax.psum(jnp.einsum('tbe,ed->tbd', part, w_out, preferred_element_type=jn...  32.9 us
    dot_general x16, matrix products, one_prompt(): jnp.einsum('hqk,khd->hqd', weights.astype(jnp.bfloat16), values_one, pref...  30.6 us
    all_gather x1, waiting for transfers between devices, shards(): lax.all_gather(text_pairs, 'seq', axis=0, tiled=True)  24.8 us
    dot_general x16, matrix products, one_prompt(): jnp.einsum('qhd,khd->hqk', query_rows, keys_one, preferred_element_type=j...  21.4 us
    reduce_scatter x1, waiting for transfers between devices, shards(): lax.psum_scatter(jnp.einsum('tbu,ud->tbd', part, w_down, preferred_elemen...  17.6 us
    slice x2, local copies, waits for them, and re-layouts, split_pairs(): pairs[..., width:].reshape(shape)  12.4 us
    all_gather x1, blocking collectives, shards(): lax.all_gather(own_hidden, 'mlp', axis=0, tiled=True).astype(jnp.float32)  11.8 us
  transfers between devices with their start and end apart: 5, of which 5 were waited for; matrix products, arithmetic and copies ran while one was open for 23% of the time, Pallas kernels for 0%

commit v1 on v0

--- a/solution.py
+++ b/solution.py
@@ -3,6 +3,8 @@
 import jax
 import jax.numpy as jnp
 from jax import lax
+from jax.experimental import pallas as pl
+from jax.experimental.pallas import tpu as pltpu
 from jax.sharding import PartitionSpec as P
 
 HEAD_DIM = 64
@@ -13,6 +15,9 @@
 EPS = 1e-06
 GUIDE = 4.5
 SHIFT = 3.0
+PROMPTS = 8
+PATCH = 64
+MESH = pl.DeviceIdType.MESH
 
 
 def partner_2(block, axis, stride):
@@ -199,6 +204,413 @@
     denoised = latent - sigma_now * velocity
     return (velocity, next_latent, denoised)
 
+def fused_kernel(
+    hid_ref, text_ref, mod_ref, len_ref, step_ref, latent_ref, wqkv_hbm, wout_hbm, wtext_hbm,
+    gain_ref, wup_hbm, wdown_hbm, whead_ref,
+    vel_ref, next_ref, den_ref,
+    wqkv, wout, wtext, wup, wdown,
+    wide, ready, gathered, normed, text_norm, q6, k6, v6, kt6, vt6, attended,
+    part, part_in, first_buf, mlp_in, act, down, down_in, final, half_out, half_in,
+    wsem, a2a_send, a2a_recv, fwd_send, fwd_recv, rs_send, rs_recv, ag_send, ag_recv,
+    dn_send, dn_recv, out_send, out_recv,
+):
+    c = lax.axis_index("cfg")
+    s = lax.axis_index("seq")
+    m = lax.axis_index("mlp")
+    other = 1 - m
+    ring = PROMPTS
+    rows = hid_ref.shape[0]
+    own_rows = rows * ring
+    width = wout.shape[0]
+    model = wout.shape[1]
+    units = wup.shape[1]
+    pairs = width // 128
+    txt_pad = text_norm.shape[0]
+    txt = text_ref.shape[0]
+    f32, bf16 = jnp.float32, jnp.bfloat16
+    partner = (c, s, other)
+
+    loads = []
+    jobs = [(wtext_hbm.at[i], wtext.at[i]) for i in range(2)]
+    jobs += [(wqkv_hbm.at[i], wqkv.at[i]) for i in range(3)]
+    jobs += [(wout_hbm, wout)]
+    jobs += [(wup_hbm.at[pl.ds(i * model // 2, model // 2)], wup.at[pl.ds(i * model // 2, model // 2)]) for i in range(2)]
+    jobs += [(wdown_hbm.at[pl.ds(i * units // 2, units // 2)], wdown.at[pl.ds(i * units // 2, units // 2)]) for i in range(2)]
+    for i, (src, dst) in enumerate(jobs):
+        loads.append(pltpu.make_async_copy(src, dst, wsem.at[i]))
+        loads[-1].start()
+
+    barrier = pltpu.get_barrier_semaphore()
+    for k in range(ring):
+        dest = lax.rem(s + k, ring)
+        if k:
+            pl.semaphore_signal(barrier, inc=1, device_id=(c, dest, m), device_id_type=MESH)
+        pl.semaphore_signal(barrier, inc=1, device_id=(1 - c, dest, m), device_id_type=MESH)
+    pl.semaphore_signal(barrier, inc=1, device_id=partner, device_id_type=MESH)
+
+    lanes = model // 128
+    for j in range(lanes):
+        tile = hid_ref[:, :, j * 128 : (j + 1) * 128]
+        wide[j] = tile.astype(f32).reshape(own_rows, 128)
+    for p in range(ring):
+        for j in range(lanes):
+            ready[p, :, j * 128 : (j + 1) * 128] = wide[j, pl.ds(p, rows, stride=ring), :].astype(bf16)
+    gathered[m, s] = ready[s]
+    pl.semaphore_wait(barrier, 2 * ring)
+
+    sends = []
+    a2a = []
+    for k in range(1, ring):
+        dest = lax.rem(s + k, ring)
+        cp = pltpu.make_async_remote_copy(
+            src_ref=ready.at[dest], dst_ref=gathered.at[m, s],
+            send_sem=a2a_send.at[k], recv_sem=a2a_recv.at[k],
+            device_id=(c, dest, m), device_id_type=MESH)
+        cp.start()
+        sends.append(cp)
+
+    def forward(k):
+        src = lax.rem(s + ring - k, ring)
+        if k:
+            pltpu.make_async_remote_copy(
+                src_ref=ready.at[src], dst_ref=gathered.at[m, src],
+                send_sem=a2a_send.at[k], recv_sem=a2a_recv.at[k],
+                device_id=(c, src, m), device_id_type=MESH).wait_recv()
+        cp = pltpu.make_async_remote_copy(
+            src_ref=gathered.at[m, src], dst_ref=gathered.at[m, src],
+            send_sem=fwd_send.at[k], recv_sem=fwd_recv.at[k],
+            device_id=partner, device_id_type=MESH)
+        cp.start()
+        sends.append(cp)
+
+    forward(0)
+
+    def mod_row(k):
+        return mod_ref[k, pl.ds(s, 1), :]
+
+    def norm_rows(values, k):
+        mean = jnp.mean(values, axis=-1, keepdims=True)
+        centred = values - mean
+        spread = jnp.mean(centred * centred, axis=-1, keepdims=True)
+        return centred * lax.rsqrt(spread + EPS) * (1.0 + mod_row(k + 1)) + mod_row(k)
+
+    whole_blocks = txt // 16
+
+    def text_block(i, carry):
+        at = pl.ds(pl.multiple_of(i * 16, 16), 16)
+        text_norm[at, :] = norm_rows(text_ref[at, :].astype(f32), 6)
+        return carry
+
+    lax.fori_loop(0, whole_blocks, text_block, 0)
+    tail = txt - whole_blocks * 16
+    if tail:
+        text_norm[whole_blocks * 16 : txt, :] = norm_rows(
+            text_ref[whole_blocks * 16 : txt, :].astype(f32), 6)
+    if txt_pad > txt:
+        text_norm[txt:txt_pad, :] = jnp.zeros((txt_pad - txt, model), f32)
+
+    forward(1)
+    forward(2)
+
+    row_id = lax.broadcasted_iota(jnp.int32, (2 * 128, 128), 0)
+    col_id = lax.broadcasted_iota(jnp.int32, (2 * 128, 128), 1)
+    same_head = (((row_id // HEAD_DIM) % 2) == (col_id // HEAD_DIM)).astype(f32).astype(bf16)
+
+    def head_norm_tile(u, gain):
+        square = u * u
+        high = square.astype(bf16)
+        low = (square - high.astype(f32)).astype(bf16)
+        total = jnp.dot(jnp.concatenate([high, low], axis=1), same_head, preferred_element_type=f32)
+        return (u * lax.rsqrt(total * (1.0 / HEAD_DIM) + EPS) * gain).astype(bf16)
+
+    def gain_of(i):
+        one = gain_ref[i : i + 1, :]
+        return jnp.concatenate([one, one], axis=1)
+
+    keep = (lax.broadcasted_iota(jnp.int32, (txt_pad, 128), 0) < len_ref[0, s]).astype(f32).astype(bf16)
+    lane = lax.broadcasted_iota(jnp.int32, (1, 128), 1)
+    low_lane = (lane < HEAD_DIM).astype(f32).astype(bf16)
+    high_lane = (lane >= HEAD_DIM).astype(f32).astype(bf16)
+
+    def project(lhs, weight, out6, gain, mask):
+        def chunk(j, carry):
+            at = pl.ds(pl.multiple_of(j * 256, 256), 256)
+            u = jnp.dot(lhs, weight[:, at], preferred_element_type=f32)
+            for t in range(2):
+                tile = u[:, t * 128 : (t + 1) * 128]
+                if gain is None:
+                    res = tile.astype(bf16)
+                else:
+                    res = head_norm_tile(tile, gain)
+                if mask is not None:
+                    res = res * mask
+                out6[2 * j + t] = res
+            return carry
+
+        lax.fori_loop(0, width // 256, chunk, 0)
+
+    text_lhs = text_norm[...].astype(bf16)
+    loads[0].wait()
+    project(text_lhs, wtext.at[0], kt6, gain_of(2), None)
+    forward(3)
+    forward(4)
+    loads[1].wait()
+    project(text_lhs, wtext.at[1], vt6, None, keep)
+    for k in range(5, ring):
+        forward(k)
+
+    def norm_half(half):
+        def block(i, carry):
+            normed[half, i] = norm_rows(gathered[half, i].astype(f32), 0).astype(bf16)
+            return carry
+
+        lax.fori_loop(0, ring, block, 0)
+
+    norm_half(m)
+    for k in range(ring):
+        src = lax.rem(s + ring - k, ring)
+        pltpu.make_async_remote_copy(
+            src_ref=gathered.at[other, src], dst_ref=gathered.at[other, src],
+            send_sem=fwd_send.at[k], recv_sem=fwd_recv.at[k],
+            device_id=partner, device_id_type=MESH).wait_recv()
+    norm_half(other)
+
+    image_lhs = normed[...].reshape(2 * own_rows, model)
+    loads[2].wait()
+    project(image_lhs, wqkv.at[0], q6, gain_of(0) * (1.0 / math.sqrt(HEAD_DIM)), None)
+    loads[3].wait()
+    project(image_lhs, wqkv.at[1], k6, gain_of(1), None)
+    loads[4].wait()
+    project(image_lhs, wqkv.at[2], v6, None, None)
+
+    def dot_t(a, b):
+        return lax.dot_general(a, b, (((1,), (1,)), ((), ())), preferred_element_type=f32)
+
+    def pair(p, carry):
+        q, k, v, kt, vt = q6[p], k6[p], v6[p], kt6[p], vt6[p]
+        outs = []
+        for mine, rest in ((low_lane, high_lane), (high_lane, low_lane)):
+            qh = q * mine
+            w_img = jnp.exp(dot_t(qh, k)).astype(bf16)
+            w_txt = jnp.exp(dot_t(qh, kt)).astype(bf16)
+            outs.append(
+                jnp.dot(w_img, v * mine + rest, preferred_element_type=f32)
+                + jnp.dot(w_txt, vt * mine + keep * rest, preferred_element_type=f32))
+        numer = jnp.where(lane < HEAD_DIM, outs[0], outs[1])
+        denom = pltpu.roll(jnp.where(lane < HEAD_DIM, outs[1], outs[0]), HEAD_DIM, 1)
+        attended[:, pl.ds(pl.multiple_of(p * 128, 128), 128)] = (numer / denom).astype(bf16)
+        return carry
+
+    lax.fori_loop(0, pairs, pair, 0)
+
+    chunks = part_in.shape[0]
+    span = model // chunks
+    loads[5].wait()
+    att = attended[...]
+    for j in range(chunks):
+        res = jnp.dot(att, wout[:, j * span : (j + 1) * span], preferred_element_type=f32).astype(bf16)
+        part[0, j] = res[:own_rows].reshape(ring, rows, span)
+        part[1, j] = res[own_rows:].reshape(ring, rows, span)
+        cp = pltpu.make_async_remote_copy(
+            src_ref=part.at[other, j], dst_ref=part_in.at[j],
+            send_sem=rs_send.at[j], recv_sem=rs_recv.at[j],
+            device_id=partner, device_id_type=MESH)
+        cp.start()
+        sends.append(cp)
+    for cp in sends[-chunks:]:
+        cp.wait_recv()
+
+    def first_block(i, carry):
+        total = jnp.concatenate(
+            [part[m, j, i].astype(f32) + part_in[j, i].astype(f32) for j in range(chunks)], axis=1)
+        first = gathered[m, i].astype(f32) + mod_row(2) * total
+        first_buf[i] = first
+        mlp_in[m, i] = norm_rows(first, 3).astype(bf16)
+        return carry
+
+    ag = []
+    for h in range(2):
+        at = pl.ds(h * ring // 2, ring // 2)
+        lax.fori_loop(h * ring // 2, (h + 1) * ring // 2, first_block, 0)
+        cp = pltpu.make_async_remote_copy(
+            src_ref=mlp_in.at[m, at], dst_ref=mlp_in.at[m, at],
+            send_sem=ag_send.at[h], recv_sem=ag_recv.at[h],
+            device_id=partner, device_id_type=MESH)
+        cp.start()
+        sends.append(cp)
+        ag.append(cp)
+
+    def up(half):
+        lhs = mlp_in[half].reshape(own_rows, model)
+
+        def chunk(j, carry):
+            at = pl.ds(pl.multiple_of(j * 512, 512), 512)
+            r = jnp.dot(lhs, wup[:, at], preferred_element_type=f32)
+            inner = math.sqrt(2.0 / math.pi) * (r + 0.044715 * (r * r * r))
+            act[half, :, at] = (0.5 * r * (1.0 + jnp.tanh(inner))).astype(bf16)
+            return carry
+
+        lax.fori_loop(0, units // 512, chunk, 0)
+
+    loads[6].wait()
+    loads[7].wait()
+    up(m)
+    for cp in ag:
+        cp.wait_recv()
+    up(other)
+    loads[8].wait()
+    loads[9].wait()
+
+    dn = []
+    for half in (other, m):
+        lhs = act[half]
+        for j in range(chunks):
+            res = jnp.dot(lhs, wdown[:, j * span : (j + 1) * span], preferred_element_type=f32)
+            down[half, j] = res.astype(bf16).reshape(ring, rows, span)
+            if len(dn) < chunks:
+                cp = pltpu.make_async_remote_copy(
+                    src_ref=down.at[other, j], dst_ref=down_in.at[j],
+                    send_sem=dn_send.at[j], recv_sem=dn_recv.at[j],
+                    device_id=partner, device_id_type=MESH)
+                cp.start()
+                sends.append(cp)
+                dn.append(cp)
+    for cp in dn:
+        cp.wait_recv()
+
+    def final_block(i, carry):
+        total = jnp.concatenate(
+            [down[m, j, i].astype(f32) + down_in[j, i].astype(f32) for j in range(chunks)], axis=1)
+        second = first_buf[i] + mod_row(5) * total
+        final[i] = norm_rows(second, 8).astype(bf16)
+        return carry
+
+    lax.fori_loop(0, ring, final_block, 0)
+    head = whead_ref[...]
+    hv = dot_t(final[...].reshape(own_rows, model), jnp.concatenate([head, head], axis=0))
+    half_out[...] = hv.reshape(ring, rows, 128)
+
+    home = s // (ring // 2)
+    slot = c * (ring // 2) + lax.rem(s, ring // 2)
+    at_home = c == home
+    for k in range(ring):
+        dest = lax.rem(s + k, ring)
+        cp = pltpu.make_async_remote_copy(
+            src_ref=half_out.at[dest], dst_ref=half_in.at[slot],
+            send_sem=out_send.at[k], recv_sem=out_recv.at[slot],
+            device_id=(home, dest, m), device_id_type=MESH)
+        if k:
+            cp.start()
+        else:
+            own = cp
+
+            @pl.when(at_home)
+            def _():
+                half_in[slot] = half_out[s]
+
+            @pl.when(jnp.logical_not(at_home))
+            def _():
+                own.start()
+
+        if k:
+            sends.append(cp)
+    for q in range(ring):
+        branch, local = q // (ring // 2), q % (ring // 2)
+        prompt = c * (ring // 2) + local
+        is_self = jnp.logical_and(c == branch, s == prompt)
+
+        @pl.when(jnp.logical_not(is_self))
+        def _():
+            pltpu.make_async_remote_copy(
+                src_ref=half_out.at[0], dst_ref=half_in.at[q],
+                send_sem=out_send.at[0], recv_sem=out_recv.at[q],
+                device_id=(branch, prompt, m), device_id_type=MESH).wait_recv()
+
+    t = step_ref[0]
+
+    def sigma(index):
+        level = 1.0 - jnp.full((1, PATCH), index, jnp.int32).astype(f32) / STEPS
+        return SHIFT * level / (1.0 + (SHIFT - 1.0) * level)
+
+    now, after = sigma(t), sigma(t + 1)
+    for p in range(ring // 2):
+        cond = half_in[p][:, :PATCH]
+        uncond = half_in[ring // 2 + p][:, :PATCH]
+        velocity = uncond + GUIDE * (cond - uncond)
+        base = latent_ref[:, p, :]
+        vel_ref[:, p, :] = velocity
+        next_ref[:, p, :] = base + (after - now) * velocity
+        den_ref[:, p, :] = base - now * velocity
+
+    for cp in sends:
+        cp.wait_send()
+
+    @pl.when(jnp.logical_not(at_home))
+    def _():
+        own.wait_send()
+
+
+def fused_shards(
+    image_hidden, text_hidden, modulation, text_lengths, timestep, latent,
+    w_qkv, w_out, w_text_kv, norm_gain, w_up, w_down, w_head,
+):
+    f32, bf16 = jnp.float32, jnp.bfloat16
+    rows, prompts, model = image_hidden.shape[1:]
+    txt = text_hidden.shape[1]
+    txt_pad = -(-txt // 16) * 16
+    width = w_out.shape[0]
+    units = w_up.shape[1]
+    own_rows = rows * prompts
+    pairs = width // 128
+    chunks = 3
+    span = model // chunks
+    vmem = pl.BlockSpec(memory_space=pltpu.VMEM)
+    smem = pl.BlockSpec(memory_space=pltpu.SMEM)
+    anym = pl.BlockSpec(memory_space=pl.ANY)
+    dma = pltpu.SemaphoreType.DMA
+    out = jax.ShapeDtypeStruct(latent.shape, f32)
+    scratch = [
+        pltpu.VMEM(w_qkv.shape, bf16), pltpu.VMEM(w_out.shape, bf16), pltpu.VMEM(w_text_kv.shape, bf16),
+        pltpu.VMEM(w_up.shape, bf16), pltpu.VMEM(w_down.shape, bf16),
+        pltpu.VMEM((model // 128, own_rows, 128), f32),
+        pltpu.VMEM((prompts, rows, model), bf16),
+        pltpu.VMEM((2, prompts, rows, model), bf16),
+        pltpu.VMEM((2, prompts, rows, model), bf16),
+        pltpu.VMEM((txt_pad, model), f32),
+        pltpu.VMEM((pairs, 2 * own_rows, 128), bf16),
+        pltpu.VMEM((pairs, 2 * own_rows, 128), bf16),
+        pltpu.VMEM((pairs, 2 * own_rows, 128), bf16),
+        pltpu.VMEM((pairs, txt_pad, 128), bf16),
+        pltpu.VMEM((pairs, txt_pad, 128), bf16),
+        pltpu.VMEM((2 * own_rows, width), bf16),
+        pltpu.VMEM((2, chunks, prompts, rows, span), bf16),
+        pltpu.VMEM((chunks, prompts, rows, span), bf16),
+        pltpu.VMEM((prompts, rows, model), f32),
+        pltpu.VMEM((2, prompts, rows, model), bf16),
+        pltpu.VMEM((2, own_rows, units), bf16),
+        pltpu.VMEM((2, chunks, prompts, rows, span), bf16),
+        pltpu.VMEM((chunks, prompts, rows, span), bf16),
+        pltpu.VMEM((prompts, rows, model), bf16),
+        pltpu.VMEM((prompts, rows, 128), f32),
+        pltpu.VMEM((prompts, rows, 128), f32),
+        dma((10,)), dma((prompts,)), dma((prompts,)), dma((prompts,)), dma((prompts,)),
+        dma((chunks,)), dma((chunks,)), dma((2,)), dma((2,)), dma((chunks,)), dma((chunks,)),
+        dma((prompts,)), dma((prompts,)),
+    ]
+    return pl.pallas_call(
+        fused_kernel,
+        out_shape=(out, out, out),
+        in_specs=[vmem, vmem, vmem, smem, smem, vmem, anym, anym, anym, vmem, anym, anym, vmem],
+        out_specs=(vmem, vmem, vmem),
+        scratch_shapes=scratch,
+        compiler_params=pltpu.CompilerParams(
+            collective_id=0, has_side_effects=True, vmem_limit_bytes=60 << 20),
+        name="fused_block",
+    )(
+        image_hidden[0], text_hidden[0], jnp.transpose(modulation[0], (1, 0, 2)), text_lengths,
+        timestep, latent, w_qkv, w_out, w_text_kv, norm_gain, w_up, w_down, jnp.transpose(w_head),
+    )
+
 
 def solution(mesh):
     placed = (
@@ -216,8 +628,9 @@
         P("mlp", None),
         P(),
     )
+    fits = mesh.shape["cfg"] == 2 and mesh.shape["seq"] == PROMPTS and mesh.shape["mlp"] == 2
     return jax.shard_map(
-        shards,
+        fused_shards if fits else shards,
         mesh=mesh,
         in_specs=placed,
         out_specs=(

time: 331 us -> 79.1 us (0.24)
  waiting for transfers between devices: 134 us -> 0 us
  matrix products: 84.1 us -> 0 us
  Pallas kernels: 0 us -> 73.3 us
  local copies, waits for them, and re-layouts: 64.2 us -> 4.12 us
  other arithmetic: 18.2 us -> 0 us
  between operations: 14.9 us -> 1.29 us
  blocking collectives: 11.8 us -> 0 us
    dot_general x43 -> x0, matrix products: 84.1 us -> none  [the longest x16 30.6 us: one_prompt(): jnp.einsum('hqk,khd->hqd', weights.astype(jnp.bfloat16), values_one, pref...]
    all_gather x2 -> x0, waiting for transfers between devices: 83.1 us -> none  [the longest x1 58.3 us: shards(): lax.all_gather(own_pairs, 'seq', axis=0, tiled=True)]
    pallas_call x0 -> x1, Pallas kernels: none -> 73.3 us  [fused_shards(): pl.pallas_call(fused_kernel, out_shape=(out, out, out), in_specs=[vmem, v...]
    psum x1 -> x0, waiting for transfers between devices: 32.9 us -> none  [shards(): lax.psum(jnp.einsum('tbe,ed->tbd', part, w_out, preferred_element_type=jn...]
    dot_general x5 -> x0, local copies, waits for them, and re-layouts: 21 us -> none  [the longest x2 9.2 us: project_image(): jnp.einsum('tbd,de->tbe', normed_rows, w_qkv[1], preferred_element_type=j...]
    reduce_scatter x1 -> x0, waiting for transfers between devices: 17.6 us -> none  [shards(): lax.psum_scatter(jnp.einsum('tbu,ud->tbd', part, w_down, preferred_elemen...]
    slice x2 -> x0, local copies, waits for them, and re-layouts: 12.4 us -> none  [split_pairs(): pairs[..., width:].reshape(shape)]
    all_gather x1 -> x0, blocking collectives: 11.8 us -> none  [shards(): lax.all_gather(own_hidden, 'mlp', axis=0, tiled=True).astype(jnp.float32)]
  transfers between devices with their start and end apart: 5 -> 0, of which waited for: 5 -> 0; matrix products, arithmetic and copies ran while one was open for 23% -> 0% of each run, Pallas kernels for 0% -> 0%
where the time goes in v1:
time: 79.1 us; the launch traced here: 78.7 us
  Pallas kernels  73.3 us (93%)
  local copies, waits for them, and re-layouts  4.12 us (5%)
  between operations  1.29 us (2%)
    pallas_call x1, Pallas kernels, fused_shards(): pl.pallas_call(fused_kernel, out_shape=(out, out, out), in_specs=[vmem, v...  73.3 us
    unnamed x3, local copies, waits for them, and re-layouts  4.12 us

profile of v1, /device:TPU:1, one launch (start us, length us, event | category | flops | bytes accessed | tf_op | source)
XLA Modules:
  0.0 78.7 jit_solution(10346753491646305285)
XLA Ops:
  1.3 73.3 %fused_block.1 = (f32[16,4,64]{2,1,0:T(4,128)}, f32[16,4,64]{2,1,0:T(4,128)}, f32[16,4,64]{2,1,0:T(4,128)}) custom-call(bf16[16,8,1536]{2,1,0:T(8,128)(2,1)} %bitcast.8, bf16[154,1536]{1,0:T(8,128)(2,1)} %bitcast.6, f32[10,8,1536]{2,1,0:T(8,128)} %bitcast.7, s32[1,8]{1,0:T(1,128)} %len_ref.1, s32[1]{0:T(128)S(6)} %copy.19.step_ref, f32[16,4,64]{2,1,0:T(4,128)} %latent_ref.1, ...), custom_call_target="tpu_custom_call" | custom-call | tf_op jit(solution)/shard_map/fused_block/pallas_call | solution.py:600
  74.6 1.4 %copy.20 = f32[16,4,64]{2,1,0:T(4,128)} copy(f32[16,4,64]{2,1,0:T(4,128)} %get-tuple-element.6) | data formatting | bytes 32768
  76.0 1.4 %copy.21 = f32[16,4,64]{2,1,0:T(4,128)} copy(f32[16,4,64]{2,1,0:T(4,128)} %get-tuple-element.7) | data formatting | bytes 32768
  77.3 1.4 %copy.22 = f32[16,4,64]{2,1,0:T(4,128)} copy(f32[16,4,64]{2,1,0:T(4,128)} %get-tuple-element.8) | data formatting | bytes 32768

commit v2 on v1

--- a/solution.py
+++ b/solution.py
@@ -207,7 +207,7 @@
 def fused_kernel(
     hid_ref, text_ref, mod_ref, len_ref, step_ref, latent_ref, wqkv_hbm, wout_hbm, wtext_hbm,
     gain_ref, wup_hbm, wdown_hbm, whead_ref,
-    vel_ref, next_ref, den_ref,
+    out_ref,
     wqkv, wout, wtext, wup, wdown,
     wide, ready, gathered, normed, text_norm, q6, k6, v6, kt6, vt6, attended,
     part, part_in, first_buf, mlp_in, act, down, down_in, final, half_out, half_in,
@@ -301,7 +301,7 @@
         text_norm[at, :] = norm_rows(text_ref[at, :].astype(f32), 6)
         return carry
 
-    lax.fori_loop(0, whole_blocks, text_block, 0)
+    lax.fori_loop(0, whole_blocks, text_block, 0, unroll=3 if whole_blocks % 3 == 0 else 1)
     tail = txt - whole_blocks * 16
     if tail:
         text_norm[whole_blocks * 16 : txt, :] = norm_rows(
@@ -332,30 +332,33 @@
     low_lane = (lane < HEAD_DIM).astype(f32).astype(bf16)
     high_lane = (lane >= HEAD_DIM).astype(f32).astype(bf16)
 
-    def project(lhs, weight, out6, gain, mask):
-        def chunk(j, carry):
-            at = pl.ds(pl.multiple_of(j * 256, 256), 256)
-            u = jnp.dot(lhs, weight[:, at], preferred_element_type=f32)
+    def project(lhs, weight, gain, mask, store):
+        for j in range(width // 256):
+            u = jnp.dot(lhs, weight[:, j * 256 : (j + 1) * 256], preferred_element_type=f32)
             for t in range(2):
                 tile = u[:, t * 128 : (t + 1) * 128]
-                if gain is None:
-                    res = tile.astype(bf16)
-                else:
-                    res = head_norm_tile(tile, gain)
-                if mask is not None:
-                    res = res * mask
-                out6[2 * j + t] = res
-            return carry
-
-        lax.fori_loop(0, width // 256, chunk, 0)
+                res = tile.astype(bf16) if gain is None else head_norm_tile(tile, gain)
+                store(2 * j + t, res if mask is None else res * mask)
+
+    def to_text(buf):
+        def store(i, value):
+            buf[i] = value
+
+        return store
+
+    def to_half(buf, half):
+        def store(i, value):
+            buf[i, half] = value
+
+        return store
 
     text_lhs = text_norm[...].astype(bf16)
     loads[0].wait()
-    project(text_lhs, wtext.at[0], kt6, gain_of(2), None)
+    project(text_lhs, wtext.at[0], gain_of(2), None, to_text(kt6))
     forward(3)
     forward(4)
     loads[1].wait()
-    project(text_lhs, wtext.at[1], vt6, None, keep)
+    project(text_lhs, wtext.at[1], None, keep, to_text(vt6))
     for k in range(5, ring):
         forward(k)
 
@@ -364,9 +367,21 @@
             normed[half, i] = norm_rows(gathered[half, i].astype(f32), 0).astype(bf16)
             return carry
 
-        lax.fori_loop(0, ring, block, 0)
+        lax.fori_loop(0, ring, block, 0, unroll=2)
+
+    q_gain = gain_of(0) * (1.0 / math.sqrt(HEAD_DIM))
+    k_gain = gain_of(1)
+
+    def image_project(half):
+        lhs = normed[half].reshape(own_rows, model)
+        project(lhs, wqkv.at[1], k_gain, None, to_half(k6, half))
+        project(lhs, wqkv.at[2], None, None, to_half(v6, half))
+        project(lhs, wqkv.at[0], q_gain, None, to_half(q6, half))
 
     norm_half(m)
+    for i in (2, 3, 4):
+        loads[i].wait()
+    image_project(m)
     for k in range(ring):
         src = lax.rem(s + ring - k, ring)
         pltpu.make_async_remote_copy(
@@ -374,146 +389,124 @@
             send_sem=fwd_send.at[k], recv_sem=fwd_recv.at[k],
             device_id=partner, device_id_type=MESH).wait_recv()
     norm_half(other)
-
-    image_lhs = normed[...].reshape(2 * own_rows, model)
-    loads[2].wait()
-    project(image_lhs, wqkv.at[0], q6, gain_of(0) * (1.0 / math.sqrt(HEAD_DIM)), None)
-    loads[3].wait()
-    project(image_lhs, wqkv.at[1], k6, gain_of(1), None)
-    loads[4].wait()
-    project(image_lhs, wqkv.at[2], v6, None, None)
+    image_project(other)
 
     def dot_t(a, b):
         return lax.dot_general(a, b, (((1,), (1,)), ((), ())), preferred_element_type=f32)
 
-    def pair(p, carry):
-        q, k, v, kt, vt = q6[p], k6[p], v6[p], kt6[p], vt6[p]
-        outs = []
-        for mine, rest in ((low_lane, high_lane), (high_lane, low_lane)):
-            qh = q * mine
-            w_img = jnp.exp(dot_t(qh, k)).astype(bf16)
-            w_txt = jnp.exp(dot_t(qh, kt)).astype(bf16)
-            outs.append(
-                jnp.dot(w_img, v * mine + rest, preferred_element_type=f32)
-                + jnp.dot(w_txt, vt * mine + keep * rest, preferred_element_type=f32))
-        numer = jnp.where(lane < HEAD_DIM, outs[0], outs[1])
-        denom = pltpu.roll(jnp.where(lane < HEAD_DIM, outs[1], outs[0]), HEAD_DIM, 1)
-        attended[:, pl.ds(pl.multiple_of(p * 128, 128), 128)] = (numer / denom).astype(bf16)
-        return carry
-
-    lax.fori_loop(0, pairs, pair, 0)
-
-    chunks = part_in.shape[0]
-    span = model // chunks
-    loads[5].wait()
-    att = attended[...]
-    for j in range(chunks):
-        res = jnp.dot(att, wout[:, j * span : (j + 1) * span], preferred_element_type=f32).astype(bf16)
-        part[0, j] = res[:own_rows].reshape(ring, rows, span)
-        part[1, j] = res[own_rows:].reshape(ring, rows, span)
+    def attend(half):
+        for p in range(pairs):
+            q, kt, vt = q6[p, half], kt6[p], vt6[p]
+            k = k6[p].reshape(2 * own_rows, 128)
+            v = v6[p].reshape(2 * own_rows, 128)
+            outs = []
+            for mine, rest in ((low_lane, high_lane), (high_lane, low_lane)):
+                qh = q * mine
+                w_img = jnp.exp(dot_t(qh, k)).astype(bf16)
+                w_txt = jnp.exp(dot_t(qh, kt)).astype(bf16)
+                outs.append(
+                    jnp.dot(w_img, v * mine + rest, preferred_element_type=f32)
+                    + jnp.dot(w_txt, vt * mine + keep * rest, preferred_element_type=f32))
+            numer = jnp.where(lane < HEAD_DIM, outs[0], outs[1])
+            denom = pltpu.roll(jnp.where(lane < HEAD_DIM, outs[1], outs[0]), HEAD_DIM, 1)
+            attended[half, :, p * 128 : (p + 1) * 128] = (numer / denom).astype(bf16)
+
+    def wide_dot(lhs, weight, out, half, first_at, count):
+        for j in range(model // 512):
+            cols = slice(j * 512, (j + 1) * 512)
+            res = jnp.dot(lhs, weight[:, cols], preferred_element_type=f32).astype(bf16)
+            out[half, first_at : first_at + count, :, cols] = res.reshape(count, rows, 512)
+
+    batches = 2
+    step = ring // batches
+
+    def swap(src, dst, send, recv, h):
+        at = pl.ds(h * step, step)
         cp = pltpu.make_async_remote_copy(
-            src_ref=part.at[other, j], dst_ref=part_in.at[j],
-            send_sem=rs_send.at[j], recv_sem=rs_recv.at[j],
+            src_ref=src.at[at], dst_ref=dst.at[at], send_sem=send.at[h], recv_sem=recv.at[h],
             device_id=partner, device_id_type=MESH)
         cp.start()
         sends.append(cp)
-    for cp in sends[-chunks:]:
-        cp.wait_recv()
+        return cp
+
+    attend(other)
+    loads[5].wait()
+    wide_dot(attended[other], wout, part, other, 0, ring)
+    rs = [swap(part.at[other], part_in, rs_send, rs_recv, h) for h in range(batches)]
+    attend(m)
+    wide_dot(attended[m], wout, part, m, 0, ring)
 
     def first_block(i, carry):
-        total = jnp.concatenate(
-            [part[m, j, i].astype(f32) + part_in[j, i].astype(f32) for j in range(chunks)], axis=1)
+        total = part[m, i].astype(f32) + part_in[i].astype(f32)
         first = gathered[m, i].astype(f32) + mod_row(2) * total
         first_buf[i] = first
         mlp_in[m, i] = norm_rows(first, 3).astype(bf16)
         return carry
 
     ag = []
-    for h in range(2):
-        at = pl.ds(h * ring // 2, ring // 2)
-        lax.fori_loop(h * ring // 2, (h + 1) * ring // 2, first_block, 0)
-        cp = pltpu.make_async_remote_copy(
-            src_ref=mlp_in.at[m, at], dst_ref=mlp_in.at[m, at],
-            send_sem=ag_send.at[h], recv_sem=ag_recv.at[h],
-            device_id=partner, device_id_type=MESH)
-        cp.start()
-        sends.append(cp)
-        ag.append(cp)
-
-    def up(half):
-        lhs = mlp_in[half].reshape(own_rows, model)
-
-        def chunk(j, carry):
-            at = pl.ds(pl.multiple_of(j * 512, 512), 512)
-            r = jnp.dot(lhs, wup[:, at], preferred_element_type=f32)
+    for h in range(batches):
+        rs[h].wait_recv()
+        lax.fori_loop(h * step, (h + 1) * step, first_block, 0, unroll=2)
+        ag.append(swap(mlp_in.at[m], mlp_in.at[m], ag_send, ag_recv, h))
+
+    def up(half, first_at, count):
+        lhs = mlp_in[half, first_at : first_at + count].reshape(count * rows, model)
+        for j in range(units // 512):
+            cols = slice(j * 512, (j + 1) * 512)
+            r = jnp.dot(lhs, wup[:, cols], preferred_element_type=f32)
             inner = math.sqrt(2.0 / math.pi) * (r + 0.044715 * (r * r * r))
-            act[half, :, at] = (0.5 * r * (1.0 + jnp.tanh(inner))).astype(bf16)
-            return carry
-
-        lax.fori_loop(0, units // 512, chunk, 0)
+            value = (0.5 * r * (1.0 + jnp.tanh(inner))).astype(bf16)
+            act[half, first_at : first_at + count, :, cols] = value.reshape(count, rows, 512)
+
+    def down_rows(half, first_at, count):
+        lhs = act[half, first_at : first_at + count].reshape(count * rows, units)
+        wide_dot(lhs, wdown, down, half, first_at, count)
 
     loads[6].wait()
     loads[7].wait()
-    up(m)
-    for cp in ag:
-        cp.wait_recv()
-    up(other)
+    up(m, 0, ring)
     loads[8].wait()
     loads[9].wait()
-
     dn = []
-    for half in (other, m):
-        lhs = act[half]
-        for j in range(chunks):
-            res = jnp.dot(lhs, wdown[:, j * span : (j + 1) * span], preferred_element_type=f32)
-            down[half, j] = res.astype(bf16).reshape(ring, rows, span)
-            if len(dn) < chunks:
-                cp = pltpu.make_async_remote_copy(
-                    src_ref=down.at[other, j], dst_ref=down_in.at[j],
-                    send_sem=dn_send.at[j], recv_sem=dn_recv.at[j],
-                    device_id=partner, device_id_type=MESH)
-                cp.start()
-                sends.append(cp)
-                dn.append(cp)
-    for cp in dn:
-        cp.wait_recv()
+    for h in range(batches):
+        ag[h].wait_recv()
+        up(other, h * step, step)
+        down_rows(other, h * step, step)
+        dn.append(swap(down.at[other], down_in, dn_send, dn_recv, h))
+    down_rows(m, 0, ring)
 
     def final_block(i, carry):
-        total = jnp.concatenate(
-            [down[m, j, i].astype(f32) + down_in[j, i].astype(f32) for j in range(chunks)], axis=1)
+        total = down[m, i].astype(f32) + down_in[i].astype(f32)
         second = first_buf[i] + mod_row(5) * total
         final[i] = norm_rows(second, 8).astype(bf16)
         return carry
 
-    lax.fori_loop(0, ring, final_block, 0)
     head = whead_ref[...]
-    hv = dot_t(final[...].reshape(own_rows, model), jnp.concatenate([head, head], axis=0))
-    half_out[...] = hv.reshape(ring, rows, 128)
-
+    heads2 = jnp.concatenate([head, head], axis=0)
     home = s // (ring // 2)
     slot = c * (ring // 2) + lax.rem(s, ring // 2)
     at_home = c == home
-    for k in range(ring):
-        dest = lax.rem(s + k, ring)
-        cp = pltpu.make_async_remote_copy(
-            src_ref=half_out.at[dest], dst_ref=half_in.at[slot],
-            send_sem=out_send.at[k], recv_sem=out_recv.at[slot],
-            device_id=(home, dest, m), device_id_type=MESH)
-        if k:
-            cp.start()
-        else:
-            own = cp
-
-            @pl.when(at_home)
-            def _():
-                half_in[slot] = half_out[s]
-
-            @pl.when(jnp.logical_not(at_home))
-            def _():
-                own.start()
-
-        if k:
-            sends.append(cp)
+    outs = []
+    for h in range(batches):
+        dn[h].wait_recv()
+        lax.fori_loop(h * step, (h + 1) * step, final_block, 0, unroll=2)
+        hv = dot_t(final[h * step : (h + 1) * step].reshape(step * rows, model), heads2)
+        half_out[h * step : (h + 1) * step] = hv.reshape(step, rows, 128)
+        for dest in range(h * step, (h + 1) * step):
+            outs.append(pltpu.make_async_remote_copy(
+                src_ref=half_out.at[dest], dst_ref=half_in.at[slot],
+                send_sem=out_send.at[dest], recv_sem=out_recv.at[slot],
+                device_id=(home, dest, m), device_id_type=MESH))
+            stays = jnp.logical_and(at_home, s == dest)
+
+            @pl.when(jnp.logical_not(stays))
+            def _(cp=outs[-1]):
+                cp.start()
+
+            @pl.when(stays)
+            def _(dest=dest):
+                half_in[slot] = half_out[dest]
+
     for q in range(ring):
         branch, local = q // (ring // 2), q % (ring // 2)
         prompt = c * (ring // 2) + local
@@ -526,10 +519,10 @@
                 send_sem=out_send.at[0], recv_sem=out_recv.at[q],
                 device_id=(branch, prompt, m), device_id_type=MESH).wait_recv()
 
-    t = step_ref[0]
+    t = step_ref[...]
 
     def sigma(index):
-        level = 1.0 - jnp.full((1, PATCH), index, jnp.int32).astype(f32) / STEPS
+        level = 1.0 - jnp.broadcast_to(index.astype(f32), (1, PATCH)) / STEPS
         return SHIFT * level / (1.0 + (SHIFT - 1.0) * level)
 
     now, after = sigma(t), sigma(t + 1)
@@ -538,16 +531,17 @@
         uncond = half_in[ring // 2 + p][:, :PATCH]
         velocity = uncond + GUIDE * (cond - uncond)
         base = latent_ref[:, p, :]
-        vel_ref[:, p, :] = velocity
-        next_ref[:, p, :] = base + (after - now) * velocity
-        den_ref[:, p, :] = base - now * velocity
+        out_ref[0, :, p, :] = velocity
+        out_ref[1, :, p, :] = base + (after - now) * velocity
+        out_ref[2, :, p, :] = base - now * velocity
 
     for cp in sends:
         cp.wait_send()
 
-    @pl.when(jnp.logical_not(at_home))
-    def _():
-        own.wait_send()
+    for dest in range(ring):
+        @pl.when(jnp.logical_not(jnp.logical_and(at_home, s == dest)))
+        def _(cp=outs[dest]):
+            cp.wait_send()
 
 
 def fused_shards(
@@ -562,13 +556,12 @@
     units = w_up.shape[1]
     own_rows = rows * prompts
     pairs = width // 128
-    chunks = 3
-    span = model // chunks
+    chunks = 2
     vmem = pl.BlockSpec(memory_space=pltpu.VMEM)
     smem = pl.BlockSpec(memory_space=pltpu.SMEM)
     anym = pl.BlockSpec(memory_space=pl.ANY)
     dma = pltpu.SemaphoreType.DMA
-    out = jax.ShapeDtypeStruct(latent.shape, f32)
+    out = jax.ShapeDtypeStruct((3,) + latent.shape, f32)
     scratch = [
         pltpu.VMEM(w_qkv.shape, bf16), pltpu.VMEM(w_out.shape, bf16), pltpu.VMEM(w_text_kv.shape, bf16),
         pltpu.VMEM(w_up.shape, bf16), pltpu.VMEM(w_down.shape, bf16),
@@ -577,19 +570,19 @@
         pltpu.VMEM((2, prompts, rows, model), bf16),
         pltpu.VMEM((2, prompts, rows, model), bf16),
         pltpu.VMEM((txt_pad, model), f32),
-        pltpu.VMEM((pairs, 2 * own_rows, 128), bf16),
-        pltpu.VMEM((pairs, 2 * own_rows, 128), bf16),
-        pltpu.VMEM((pairs, 2 * own_rows, 128), bf16),
+        pltpu.VMEM((pairs, 2, own_rows, 128), bf16),
+        pltpu.VMEM((pairs, 2, own_rows, 128), bf16),
+        pltpu.VMEM((pairs, 2, own_rows, 128), bf16),
         pltpu.VMEM((pairs, txt_pad, 128), bf16),
         pltpu.VMEM((pairs, txt_pad, 128), bf16),
-        pltpu.VMEM((2 * own_rows, width), bf16),
-        pltpu.VMEM((2, chunks, prompts, rows, span), bf16),
-        pltpu.VMEM((chunks, prompts, rows, span), bf16),
+        pltpu.VMEM((2, own_rows, width), bf16),
+        pltpu.VMEM((2, prompts, rows, model), bf16),
+        pltpu.VMEM((prompts, rows, model), bf16),
         pltpu.VMEM((prompts, rows, model), f32),
         pltpu.VMEM((2, prompts, rows, model), bf16),
-        pltpu.VMEM((2, own_rows, units), bf16),
-        pltpu.VMEM((2, chunks, prompts, rows, span), bf16),
-        pltpu.VMEM((chunks, prompts, rows, span), bf16),
+        pltpu.VMEM((2, prompts, rows, units), bf16),
+        pltpu.VMEM((2, prompts, rows, model), bf16),
+        pltpu.VMEM((prompts, rows, model), bf16),
         pltpu.VMEM((prompts, rows, model), bf16),
         pltpu.VMEM((prompts, rows, 128), f32),
         pltpu.VMEM((prompts, rows, 128), f32),
@@ -597,19 +590,20 @@
         dma((chunks,)), dma((chunks,)), dma((2,)), dma((2,)), dma((chunks,)), dma((chunks,)),
         dma((prompts,)), dma((prompts,)),
     ]
-    return pl.pallas_call(
+    stacked = pl.pallas_call(
         fused_kernel,
-        out_shape=(out, out, out),
-        in_specs=[vmem, vmem, vmem, smem, smem, vmem, anym, anym, anym, vmem, anym, anym, vmem],
-        out_specs=(vmem, vmem, vmem),
+        out_shape=out,
+        in_specs=[vmem, vmem, vmem, smem, vmem, vmem, anym, anym, anym, vmem, anym, anym, vmem],
+        out_specs=vmem,
         scratch_shapes=scratch,
         compiler_params=pltpu.CompilerParams(
             collective_id=0, has_side_effects=True, vmem_limit_bytes=60 << 20),
         name="fused_block",
     )(
         image_hidden[0], text_hidden[0], jnp.transpose(modulation[0], (1, 0, 2)), text_lengths,
-        timestep, latent, w_qkv, w_out, w_text_kv, norm_gain, w_up, w_down, jnp.transpose(w_head),
-    )
+        timestep.reshape(1, 1), latent, w_qkv, w_out, w_text_kv, norm_gain, w_up, w_down, jnp.transpose(w_head),
+    )
+    return stacked[0], stacked[1], stacked[2]
 
 
 def solution(mesh):

time: 79.1 us -> 63.6 us (0.80)
  Pallas kernels: 73.3 us -> 60.4 us
  local copies, waits for them, and re-layouts: 4.12 us -> 1.43 us
    pallas_call x1, Pallas kernels: 73.3 us -> 60.4 us  [fused_shards(): pl.pallas_call(fused_kernel, out_shape=out, in_specs=[vmem, vmem, vmem, s...]
    unnamed x3 -> x0, local copies, waits for them, and re-layouts: 4.12 us -> none
    squeeze x0 -> x1, local copies, waits for them, and re-layouts: none -> 1.43 us  [fused_shards(): return (stacked[0], stacked[1], stacked[2])]
where the time goes in v2:
time: 63.6 us; the launch traced here: 63.1 us
  Pallas kernels  60.4 us (95%)
  local copies, waits for them, and re-layouts  1.43 us (2%)
  between operations  1.29 us (2%)
    pallas_call x1, Pallas kernels, fused_shards(): pl.pallas_call(fused_kernel, out_shape=out, in_specs=[vmem, vmem, vmem, s...  60.4 us
    squeeze x1, local copies, waits for them, and re-layouts, fused_shards(): return (stacked[0], stacked[1], stacked[2])  1.43 us

profile of v2, /device:TPU:1, one launch (start us, length us, event | category | flops | bytes accessed | tf_op | source)
XLA Modules:
  0.0 63.1 jit_solution(2432144854902768247)
XLA Ops:
  1.3 60.4 %fused_block.1 = f32[3,16,4,64]{3,2,1,0:T(4,128)} custom-call(bf16[16,8,1536]{2,1,0:T(8,128)(2,1)} %bitcast.16, bf16[154,1536]{1,0:T(8,128)(2,1)} %bitcast.14, f32[10,8,1536]{2,1,0:T(8,128)} %bitcast.15, s32[1,8]{1,0:T(1,128)} %len_ref.1, s32[1,1]{1,0:T(1,128)} %bitcast.13.step_ref, f32[16,4,64]{2,1,0:T(4,128)} %latent_ref.1, ...), custom_call_target="tpu_custom_call" | custom-call | tf_op jit(solution)/shard_map/fused_block/pallas_call | solution.py:593
  61.7 1.4 %slice_bitcast_fusion = (f32[16,4,64]{2,1,0:T(4,128)}, f32[16,4,64]{2,1,0:T(4,128)}, f32[16,4,64]{2,1,0:T(4,128)}) fusion(f32[3,16,4,64]{3,2,1,0:T(4,128)} %fused_block.1), kind=kLoop, calls=%fused_computation | loop fusion | bytes 98304 | tf_op jit(solution)/shard_map/squeeze | solution.py:606
